TPU v7x, 512 devices: a whole 4x8x8 slice. The times are simulated.
512 devices in a mesh: panel: 2 (over x_hi), rad: 8 (over z), ang: 32 (over y, x_lo, core).
Axes of the slice: x: 4 (x_hi: 2, x_lo: 2; x = x_hi * 2 + x_lo), y: 8, z: 8, core: 2. Of those that a mesh axis runs over, the one named last changes fastest.
Arguments:
- adj_final: float32 [2, 7, 8, 256, 1536], P('panel', None, 'rad', 'ang'), may hold values from -6 to 6
- cond: float32 [2, 8, 256, 1536], P('panel', 'rad', 'ang'), may hold values from 0.5 to 1.5
- diffus: float32 [7], replicated, may hold values from 0.02 to 0.1
- couple: float32 [7, 7], replicated, may hold values from -0.1 to 0.1
- ghost_row: int32 [2, 4, 256], replicated, may hold values from 0 to 255
- ghost_col: int32 [2, 4, 256], replicated, may hold values from 0 to 1535
- ghost_wt: float32 [2, 4, 256], replicated, may hold values from 0.5 to 1.5
- obs_dest: int32 [2, 8, 8192, 1], P('panel', 'rad', 'ang'), may hold values from 0 to 31; in each aligned block of 256 rows (0 to 255, 256 to 511, ..., all dimensions but the last counted through in order) at most 16 rows name the same one
- obs_cell: int32 [2, 8, 4, 8192], P('panel', 'rad', None, 'ang'), may hold values from 0 to 12287
- obs_wt: float32 [2, 8, 4, 8192], P('panel', 'rad', None, 'ang'), may hold values from 0.2 to 1
- misfit: float32 [2, 8, 2, 8192], P('panel', 'rad', None, 'ang'), may hold values from -6 to 6
Outputs:
- adj_start: float32 [2, 7, 8, 256, 1536], P('panel', None, 'rad', 'ang')
Inputs may be any that keep to these rules, and one draw needn't show every extreme that they name: `obs_dest`: owner tile, within the observation's own panel, whose outermost layer holds it; among the 256 observations of one device at most 16 name one owner. `obs_cell`: row within the owner's tile times 1536 plus column.
All inputs are finite; a program needn't handle non-finite values.
Results may differ from a plain program's by a relative error of at most 0.000088.
Values sent between devices are 32-bit elements; how exact they have to be, the bound alone decides.
A program may use at most 64 MiB of HBM per device.

v0:
```python
import jax
import jax.numpy as jnp
from jax import lax
from jax.sharding import PartitionSpec as P


def swapped(x, axis, apart):
    return lax.ppermute(x, axis, [(i, i ^ 1 << apart) for i in range(lax.axis_size(axis))])


def extended(block, sides, width):
    for axis, dim in sides:
        count = lax.axis_size(axis)
        forward = [(i, i + 1) for i in range(count - 1)]
        backward = [(target, source) for source, target in forward]
        low = lax.ppermute(
            lax.slice_in_dim(block, block.shape[dim] - width, None, axis=dim), axis, forward
        )
        high = lax.ppermute(lax.slice_in_dim(block, 0, width, axis=dim), axis, backward)
        block = jnp.concatenate([low, block, high], axis=dim)
    return block


def deposit(inbox, cells_total):
    values = inbox[:8].reshape(2, -1)
    cells = inbox[8:].astype(jnp.int32).reshape(-1)
    dense = jnp.zeros((2, cells_total), jnp.float32)
    return dense.at[:, cells].add(values, mode="drop")


def route_obs(obs_dest, obs_cell, obs_wt, misfit, cells_total):
    target = obs_dest[0, 0, :, 0]
    count = target.shape[0]
    owners = lax.axis_size("ang")
    slots = 2 * count // owners
    onehot = (target[:, None] == jnp.arange(owners, dtype=jnp.int32)[None]).astype(jnp.int32)
    before = jnp.cumsum(onehot, axis=0) - onehot
    ranking = jnp.sum(before * onehot, axis=1)
    position = target * slots + ranking
    values = (misfit[0, 0][:, None, :] * obs_wt[0, 0][None]).reshape(8, count)
    payload = jnp.concatenate([values, obs_cell[0, 0].astype(jnp.float32)], axis=0)
    blank = jnp.concatenate(
        [
            jnp.zeros((8, owners * slots), jnp.float32),
            jnp.full((4, owners * slots), cells_total, jnp.float32),
        ],
        axis=0,
    )
    outbox = blank.at[:, position].set(payload)
    inbox = lax.all_to_all(outbox, "ang", split_axis=1, concat_axis=1, tiled=True)
    dense = deposit(inbox, cells_total)
    return lax.psum(dense, "rad")


def other_edges(edges):
    across = swapped(edges, "panel", 0)
    return lax.all_gather(across, "ang", axis=3, tiled=True)


def ghost_terms(scaled_own, row_start, central_rows, ghost_row, ghost_col, ghost_wt):
    fields, layers, tile_rows, columns = scaled_own.shape
    edges = jnp.stack([scaled_own[..., 0], scaled_own[..., -1]], axis=2)
    gathered = other_edges(edges)
    values = gathered[:, :, :, None, :] * ghost_wt[None, None]
    local_row = ghost_row - row_start
    inside = (local_row >= 0) & (local_row < central_rows)
    flat_index = jnp.where(inside, local_row * columns + ghost_col, central_rows * columns).reshape(
        -1
    )
    target = jnp.zeros((fields, layers, central_rows * columns), jnp.float32)
    target = target.at[:, :, flat_index].add(values.reshape(fields, layers, -1), mode="drop")
    return target.reshape(fields, layers, central_rows, columns)


def finish(padded, centre, ghost_add, source, couple, row_start, total_rows):
    middle = padded[:, 1:-1, 1:-1]
    lap = padded[:, 2:, 1:-1] + padded[:, :-2, 1:-1] + padded[:, 1:-1, 2:] + padded[:, 1:-1, :-2]
    west = jnp.pad(middle[..., :-1], ((0, 0), (0, 0), (0, 0), (1, 0)))
    east = jnp.pad(middle[..., 1:], ((0, 0), (0, 0), (0, 0), (0, 1)))
    lap = lap + west + east - 6.0 * middle
    coupled = jnp.einsum("ec,elrk->clrk", couple, centre, precision=lax.Precision.HIGHEST)
    updated = centre + lap + ghost_add + coupled
    updated = updated.at[3].add(source)
    global_rows = row_start + jnp.arange(centre.shape[2], dtype=jnp.int32)
    inside = ((global_rows >= 0) & (global_rows < total_rows)).astype(jnp.float32)
    return updated * inside[None, None, :, None]


def shallow_step(
    adjoint, coeff, source, couple, row_start, total_rows, ghost_row, ghost_col, ghost_wt
):
    scaled = coeff * adjoint
    padded = extended(scaled, (("rad", 1), ("ang", 2)), 1)
    ghost_add = ghost_terms(scaled, row_start, adjoint.shape[2], ghost_row, ghost_col, ghost_wt)
    return finish(padded, adjoint, ghost_add, source, couple, row_start, total_rows)


def body(
    adj_final,
    cond,
    diffus,
    couple,
    ghost_row,
    ghost_col,
    ghost_wt,
    obs_dest,
    obs_cell,
    obs_wt,
    misfit,
):
    adjoint = adj_final[0]
    conduct = cond[0]
    fields, layers, tile_rows, columns = adjoint.shape
    total_rows = tile_rows * lax.axis_size("ang")
    row_start = lax.axis_index("ang") * tile_rows
    outer = (lax.axis_index("rad") == lax.axis_size("rad") - 1).astype(jnp.float32)
    forcing = route_obs(obs_dest, obs_cell, obs_wt, misfit, tile_rows * columns)
    sources = []
    for moment in range(2):
        blank = jnp.zeros((layers, tile_rows, columns), jnp.float32)
        sources.append(
            blank.at[layers - 1].set(forcing[moment].reshape(tile_rows, columns) * outer)
        )
    coeff = diffus[:, None, None, None] * conduct[None]
    first = shallow_step(
        adjoint, coeff, sources[1], couple, row_start, total_rows, ghost_row, ghost_col, ghost_wt
    )
    final = shallow_step(
        first, coeff, sources[0], couple, row_start, total_rows, ghost_row, ghost_col, ghost_wt
    )
    return final[None]


def solution(mesh):
    placed = (
        P("panel", None, "rad", "ang", None),
        P("panel", "rad", "ang", None),
        P(),
        P(),
        P(),
        P(),
        P(),
        P("panel", "rad", "ang", None),
        P("panel", "rad", None, "ang"),
        P("panel", "rad", None, "ang"),
        P("panel", "rad", None, "ang"),
    )
    return jax.shard_map(
        body,
        mesh=mesh,
        in_specs=placed,
        out_specs=P("panel", None, "rad", "ang", None),
        check_vma=False,
    )
```

profile of v0, /device:TPU:1, one launch (start us, length us, event | category | flops | bytes accessed | tf_op | source)
XLA Modules:
  0.0 364.4 jit_solution(14950490070713340924)
XLA Ops:
  6.5 1.2 multiply_multiply_fusion.1
  7.8 1.3 collective-permute-start
  9.1 5.5 %collective-permute-start.1 = (f32[7,1,8,1536]{3,0,2,1:T(8,128)S(1)}, f32[7,1,8,1536]{3,0,2,1:T(8,128)S(1)}, u32[]{:S(2)}, u32[]{:S(2)}) collective-permute-start(f32[7,1,8,1536]{3,0,2,1:T(8,128)S(1)} %multiply_multiply_fusion.1), channel_id=1, source_target_pairs={{0,32},{32,64},{64,96},{96,128},{128,160},{160,192},{192,224},{1,3... | collective-permute-start | bytes 1032200 | tf_op jit(solution)/shard_map/ppermute | solution.py:16
  14.6 0.1 copy.73
  14.8 0.1 copy.74
  14.9 4.7 %collective-permute-start.4 = (f32[7,1,2,8]{3,2,0,1:T(2,128)S(1)}, f32[7,1,2,8]{3,2,0,1:T(2,128)S(1)}, u32[]{:S(2)}, u32[]{:S(2)}) collective-permute-start(f32[7,1,2,8]{3,2,0,1:T(2,128)S(1)} %pad_maximum_fusion.18), channel_id=1, source_target_pairs={{0,256},{256,0},{1,257},{257,1},{2,258},{258,2},{3,259},{259,3},{4... | collective-permute-start | bytes 1352 | tf_op jit(solution)/shard_map/ppermute | solution.py:8
  19.6 0.7 fusion.37
  20.3 0.6 reduce-window.6
  20.8 0.2 slice_reduce_fusion
  21.1 0.8 fusion.36
  21.8 0.7 compare_select_fusion.2
  22.5 0.9 copy.119
  23.5 0.7 broadcast_multiply_fusion
  24.2 0.7 convert_bitcast_fusion
  24.9 0.1 copy.82
  25.0 1.3 scatter_fusion
  26.3 0.3 copy.83
  26.5 0.8 reshape.458
  27.3 8.5 %all-to-all-start = ((f32[32,1,192]{2,1,0:T(1,128)}), f32[32,1,192]{2,1,0:T(1,128)S(1)}, u32[]{:S(2)}, u32[]{:S(2)}) async-start(f32[32,1,192]{2,1,0:T(1,128)} %reshape.458), calls=%async_computation | async-start | bytes 65536 | tf_op jit(solution)/shard_map/all_to_all | solution.py:50
  35.9 0.2 fusion.42
  36.1 0.7 add_select_fusion
  36.9 0.7 copy.108
  37.6 0.1 copy.75
  37.7 35.1 %all_gather.6 = f32[7,1,2,256]{0,2,1,3:T(2,128)S(1)} all-gather(f32[7,1,2,8]{0,2,1,3:T(2,128)S(1)} %copy.75), channel_id=1, replica_groups=mesh['panel'=2,'rad'=8,'ang'=32] {'ang'}, dimensions={3}, use_global_device_ids=true | all-gather | bytes 14784 | tf_op jit(solution)/shard_map/all_gather | solution.py:57
  72.8 15.5 %scatter_custom_fusion = f32[7,12288]{0,1:T(8,128)} fusion(s32[2048]{0:T(1024)S(1)} %bitcast.114, f32[]{:T(128)} %constant.119.clone.1, f32[7,1,2048]{0,2,1:T(8,128)S(1)} %bitcast.92, f32[2048]{0:T(1024)S(1)} %bitcast.104), kind=kCustom, calls=%fused_computation.10 | custom fusion | flops 28672 | bytes 1400836 | tf_op jit(solution)/shard_map/scatter-add | solution.py:71
  88.3 4.4 %copy.78 = f32[7,1,8,1536]{3,0,2,1:T(8,128)S(1)} copy(f32[7,1,8,1536]{0,3,2,1:T(8,128)} %bitcast.90) | data formatting | bytes 688128 | tf_op jit(solution)/shard_map/reshape | solution.py:72
  92.8 0.5 broadcast.324
  93.3 0.7 reduce.14
  94.0 0.1 reshape.459
  94.2 0.1 reshape.428
  94.3 1.4 copy.87
  95.8 0.1 copy.85
  95.9 0.1 convert_element_type.51
  96.0 14.8 %scatter_custom_fusion.2 = f32[2,12288]{0,1:T(8,128)} fusion(s32[2048]{0:T(1024)S(1)} %bitcast.116, f32[2048,2]{1,0:T(8,128)} %copy.87, f32[]{:T(128)} %constant.119.clone.1), kind=kCustom, calls=%fused_computation.12 | custom fusion | flops 4096 | bytes 98816 | tf_op jit(solution)/shard_map/scatter-add | solution.py:28
  110.9 0.7 pad_maximum_fusion.17
  111.6 2.1 collective-permute-start.2
  113.7 3.8 %collective-permute-start.3 = (f32[7,3,1,1536]{3,0,2,1:T(8,128)S(1)}, f32[7,3,1,1536]{3,0,2,1:T(8,128)S(1)}, u32[]{:S(2)}, u32[]{:S(2)}) collective-permute-start(f32[7,3,1,1536]{3,0,2,1:T(8,128)S(1)} %get-tuple-element.58), channel_id=1, source_target_pairs={{0,1},{1,2},{2,3},{3,4},{4,5},{5,6},{6,7},{7,8},{8,9},{9,10},{10,1... | collective-permute-start | bytes 387080 | tf_op jit(solution)/shard_map/ppermute | solution.py:16
  117.5 148.5 %all-reduce.6.cloned.1.call-done = f32[2,12288]{0,1:T(8,128)} async-done(((f32[2,12288]{0,1:T(8,128)}), f32[2,12288]{0,1:T(8,128)}) %all-reduce.6.cloned.1.call-update) | async-done | bytes 98320 | tf_op jit(solution)/shard_map/psum | solution.py:52
  266.0 9.6 %fusion = (f32[12288]{0:T(1024)S(1)}, f32[12288]{0:T(1024)S(1)}) fusion(f32[2,12288]{0,1:T(8,128)} %all-reduce.6.cloned.1.call-done, f32[]{:T(128)S(6)} %convert_element_type.52), kind=kLoop, calls=%fused_computation.5 | loop fusion | flops 24576 | bytes 196612 | tf_op jit(solution)/shard_map/mul | solution.py:122
  275.7 0.7 copy-done.3
  276.4 1.9 fusion.9
  278.2 0.1 slice_add_fusion.1
  278.3 0.6 scatter-add.33
  278.9 0.1 multiply_multiply_fusion
  279.0 1.3 collective-permute-start.5
  280.3 4.0 %collective-permute-start.6 = (f32[7,1,8,1536]{3,0,2,1:T(8,128)S(1)}, f32[7,1,8,1536]{3,0,2,1:T(8,128)S(1)}, u32[]{:S(2)}, u32[]{:S(2)}) collective-permute-start(f32[7,1,8,1536]{3,0,2,1:T(8,128)S(1)} %multiply_multiply_fusion), channel_id=1, source_target_pairs={{0,32},{32,64},{64,96},{96,128},{128,160},{160,192},{192,224},{1,3... | collective-permute-start | bytes 1032200 | tf_op jit(solution)/shard_map/ppermute | solution.py:16
  284.4 0.1 copy.89
  284.5 0.1 copy.90
  284.7 4.6 %collective-permute-start.9 = (f32[7,1,2,8]{3,2,0,1:T(2,128)S(1)}, f32[7,1,2,8]{3,2,0,1:T(2,128)S(1)}, u32[]{:S(2)}, u32[]{:S(2)}) collective-permute-start(f32[7,1,2,8]{3,2,0,1:T(2,128)S(1)} %pad_maximum_fusion.19), channel_id=1, source_target_pairs={{0,256},{256,0},{1,257},{257,1},{2,258},{258,2},{3,259},{259,3},{4... | collective-permute-start | bytes 1352 | tf_op jit(solution)/shard_map/ppermute | solution.py:8
  289.3 1.6 collective-permute-done.5
  290.9 0.9 collective-permute-done.6
  291.8 0.7 pad_maximum_fusion.14
  292.5 3.8 %collective-permute-start.7 = (f32[7,3,1,1536]{3,0,2,1:T(8,128)}, f32[7,3,1,1536]{3,0,2,1:T(8,128)}, u32[]{:S(2)}, u32[]{:S(2)}) collective-permute-start(f32[7,3,1,1536]{3,0,2,1:T(8,128)} %get-tuple-element.55), channel_id=1, source_target_pairs={{1,0},{2,1},{3,2},{4,3},{5,4},{6,5},{7,6},{8,7},{9,8},{10,9},{11,1... | collective-permute-start | bytes 387080 | tf_op jit(solution)/shard_map/ppermute | solution.py:19
  296.3 3.0 collective-permute-start.8
  299.3 0.2 fusion.40
  299.4 0.1 copy.91
  299.5 34.7 %all_gather.7 = f32[7,1,2,256]{0,2,1,3:T(2,128)S(1)} all-gather(f32[7,1,2,8]{0,2,1,3:T(2,128)S(1)} %copy.91), channel_id=1, replica_groups=mesh['panel'=2,'rad'=8,'ang'=32] {'ang'}, dimensions={3}, use_global_device_ids=true | all-gather | bytes 14784 | tf_op jit(solution)/shard_map/all_gather | solution.py:57
  334.3 15.5 %scatter_custom_fusion.3 = f32[7,12288]{0,1:T(8,128)} fusion(s32[2048]{0:T(1024)S(1)} %bitcast.115, f32[]{:T(128)} %constant.119.clone.1, f32[7,1,2048]{0,2,1:T(8,128)S(1)} %bitcast.91, f32[2048]{0:T(1024)S(1)} %bitcast.105), kind=kCustom, calls=%fused_computation.8 | custom fusion | flops 28672 | bytes 1400836 | tf_op jit(solution)/shard_map/scatter-add | solution.py:71
  349.8 4.4 %copy.94 = f32[7,1,8,1536]{3,0,2,1:T(8,128)S(1)} copy(f32[7,1,8,1536]{0,3,2,1:T(8,128)} %bitcast.89) | data formatting | bytes 688128 | tf_op jit(solution)/shard_map/reshape | solution.py:72
  354.3 1.6 fusion.8
  355.9 0.1 slice_add_fusion
  355.9 0.6 scatter-add.35
  356.5 0.1 multiply_bitcast_fusion
  356.6 0.9 copy.97
  (41 shorter events, 0.7 us)
Async XLA Ops:
  6.5 269.8 %copy-start = (f32[7,7]{1,0:T(8,128)S(1)}, f32[7,7]{1,0:T(8,128)}, u32[]{:S(2)}) copy-start(f32[7,7]{1,0:T(8,128)} %param.22) | copy-start | bytes 592
  7.8 103.1 %collective-permute-start = (f32[7,1,8,1536]{3,0,2,1:T(8,128)S(1)}, f32[7,1,8,1536]{3,0,2,1:T(8,128)S(1)}, u32[]{:S(2)}, u32[]{:S(2)}) collective-permute-start(f32[7,1,8,1536]{3,0,2,1:T(8,128)S(1)} %multiply_multiply_fusion.1), channel_id=1, source_target_pairs={{32,0},{64,32},{96,64},{128,96},{160,128},{192,160},{224,192},{33,... | collective-permute-start | bytes 1032200 | tf_op jit(solution)/shard_map/ppermute | solution.py:19
  9.1 101.8 %collective-permute-start.1 = (f32[7,1,8,1536]{3,0,2,1:T(8,128)S(1)}, f32[7,1,8,1536]{3,0,2,1:T(8,128)S(1)}, u32[]{:S(2)}, u32[]{:S(2)}) collective-permute-start(f32[7,1,8,1536]{3,0,2,1:T(8,128)S(1)} %multiply_multiply_fusion.1), channel_id=1, source_target_pairs={{0,32},{32,64},{64,96},{96,128},{128,160},{160,192},{192,224},{1,3... | collective-permute-start | bytes 1032200 | tf_op jit(solution)/shard_map/ppermute | solution.py:16
  14.9 22.7 %collective-permute-start.4 = (f32[7,1,2,8]{3,2,0,1:T(2,128)S(1)}, f32[7,1,2,8]{3,2,0,1:T(2,128)S(1)}, u32[]{:S(2)}, u32[]{:S(2)}) collective-permute-start(f32[7,1,2,8]{3,2,0,1:T(2,128)S(1)} %pad_maximum_fusion.18), channel_id=1, source_target_pairs={{0,256},{256,0},{1,257},{257,1},{2,258},{258,2},{3,259},{259,3},{4... | collective-permute-start | bytes 1352 | tf_op jit(solution)/shard_map/ppermute | solution.py:8
  27.3 65.4 %all-to-all-start = ((f32[32,1,192]{2,1,0:T(1,128)}), f32[32,1,192]{2,1,0:T(1,128)S(1)}, u32[]{:S(2)}, u32[]{:S(2)}) async-start(f32[32,1,192]{2,1,0:T(1,128)} %reshape.458), calls=%async_computation | async-start | bytes 65536 | tf_op jit(solution)/shard_map/all_to_all | solution.py:50
  35.9 230.2 %all-reduce.6.cloned.1.call-start = ((), (), s32[]{:S(2)}) async-start(), calls=%async_computation.1 | async-start | bytes 12582912 | tf_op jit(solution)/shard_map/psum | solution.py:52
  111.6 164.1 %collective-permute-start.2 = (f32[7,3,1,1536]{3,0,2,1:T(8,128)}, f32[7,3,1,1536]{3,0,2,1:T(8,128)S(1)}, u32[]{:S(2)}, u32[]{:S(2)}) collective-permute-start(f32[7,3,1,1536]{3,0,2,1:T(8,128)} %get-tuple-element.57), channel_id=1, source_target_pairs={{1,0},{2,1},{3,2},{4,3},{5,4},{6,5},{7,6},{8,7},{9,8},{10,9},{11,1... | collective-permute-start | bytes 387080 | tf_op jit(solution)/shard_map/ppermute | solution.py:19
  113.7 162.7 %copy-start.1 = (f32[1,7,1,8,1536]{4,3,2,1,0:T(8,128)S(1)}, f32[1,7,1,8,1536]{4,3,2,1,0:T(8,128)}, u32[]{:S(2)}) copy-start(f32[1,7,1,8,1536]{4,3,2,1,0:T(8,128)} %param.19) | copy-start | bytes 1032196
  113.7 165.2 %copy-start.2 = (f32[1,1,8,1536]{3,2,1,0:T(8,128)S(1)}, f32[1,1,8,1536]{3,2,1,0:T(8,128)}, u32[]{:S(2)}) copy-start(f32[1,1,8,1536]{3,2,1,0:T(8,128)} %param.20) | copy-start | bytes 147460
  113.7 165.2 %copy-start.4 = (f32[7]{0:T(128)S(1)}, f32[7]{0:T(128)}, u32[]{:S(2)}) copy-start(f32[7]{0:T(128)} %param.21) | copy-start | bytes 88
  113.7 162.0 %collective-permute-start.3 = (f32[7,3,1,1536]{3,0,2,1:T(8,128)S(1)}, f32[7,3,1,1536]{3,0,2,1:T(8,128)S(1)}, u32[]{:S(2)}, u32[]{:S(2)}) collective-permute-start(f32[7,3,1,1536]{3,0,2,1:T(8,128)S(1)} %get-tuple-element.58), channel_id=1, source_target_pairs={{0,1},{1,2},{2,3},{3,4},{4,5},{5,6},{6,7},{7,8},{8,9},{9,10},{10,1... | collective-permute-start | bytes 387080 | tf_op jit(solution)/shard_map/ppermute | solution.py:16
  275.7 0.7 copy-start.3
  279.0 11.9 %collective-permute-start.5 = (f32[7,1,8,1536]{3,0,2,1:T(8,128)S(1)}, f32[7,1,8,1536]{3,0,2,1:T(8,128)S(1)}, u32[]{:S(2)}, u32[]{:S(2)}) collective-permute-start(f32[7,1,8,1536]{3,0,2,1:T(8,128)S(1)} %multiply_multiply_fusion), channel_id=1, source_target_pairs={{32,0},{64,32},{96,64},{128,96},{160,128},{192,160},{224,192},{33,... | collective-permute-start | bytes 1032200 | tf_op jit(solution)/shard_map/ppermute | solution.py:19
  280.3 11.4 %collective-permute-start.6 = (f32[7,1,8,1536]{3,0,2,1:T(8,128)S(1)}, f32[7,1,8,1536]{3,0,2,1:T(8,128)S(1)}, u32[]{:S(2)}, u32[]{:S(2)}) collective-permute-start(f32[7,1,8,1536]{3,0,2,1:T(8,128)S(1)} %multiply_multiply_fusion), channel_id=1, source_target_pairs={{0,32},{32,64},{64,96},{96,128},{128,160},{160,192},{192,224},{1,3... | collective-permute-start | bytes 1032200 | tf_op jit(solution)/shard_map/ppermute | solution.py:16
  284.7 14.8 %collective-permute-start.9 = (f32[7,1,2,8]{3,2,0,1:T(2,128)S(1)}, f32[7,1,2,8]{3,2,0,1:T(2,128)S(1)}, u32[]{:S(2)}, u32[]{:S(2)}) collective-permute-start(f32[7,1,2,8]{3,2,0,1:T(2,128)S(1)} %pad_maximum_fusion.19), channel_id=1, source_target_pairs={{0,256},{256,0},{1,257},{257,1},{2,258},{258,2},{3,259},{259,3},{4... | collective-permute-start | bytes 1352 | tf_op jit(solution)/shard_map/ppermute | solution.py:8
  292.5 61.8 %collective-permute-start.7 = (f32[7,3,1,1536]{3,0,2,1:T(8,128)}, f32[7,3,1,1536]{3,0,2,1:T(8,128)}, u32[]{:S(2)}, u32[]{:S(2)}) collective-permute-start(f32[7,3,1,1536]{3,0,2,1:T(8,128)} %get-tuple-element.55), channel_id=1, source_target_pairs={{1,0},{2,1},{3,2},{4,3},{5,4},{6,5},{7,6},{8,7},{9,8},{10,9},{11,1... | collective-permute-start | bytes 387080 | tf_op jit(solution)/shard_map/ppermute | solution.py:19
  296.3 58.0 %collective-permute-start.8 = (f32[7,3,1,1536]{3,0,2,1:T(8,128)}, f32[7,3,1,1536]{3,0,2,1:T(8,128)}, u32[]{:S(2)}, u32[]{:S(2)}) collective-permute-start(f32[7,3,1,1536]{3,0,2,1:T(8,128)} %get-tuple-element.56), channel_id=1, source_target_pairs={{0,1},{1,2},{2,3},{3,4},{4,5},{5,6},{6,7},{7,8},{8,9},{9,10},{10,1... | collective-permute-start | bytes 387080 | tf_op jit(solution)/shard_map/ppermute | solution.py:16
Sparse Core Ops, SparseCore 0:
  111.0 154.9 all-reduce.5
where the time goes:
time: 365 us; the launch traced here: 364 us
  waiting for transfers between devices  151 us (41%)
  blocking collectives  69.8 us (19%)
  other arithmetic  64.2 us (18%)
  starting transfers between devices  42.5 us (12%)
  local copies, waits for them, and re-layouts  19.7 us (5%)
  between operations  13.8 us (4%)
    psum x1, waiting for transfers between devices, route_obs(): return lax.psum(dense, 'rad')  149 us
    all_gather x2, blocking collectives, other_edges(): return lax.all_gather(across, 'ang', axis=3, tiled=True)  69.8 us
    scatter-add x2, other arithmetic, ghost_terms(): target.at[:, :, flat_index]  31 us
    ppermute x4, starting transfers between devices, extended(): lax.ppermute(lax.slice_in_dim(block, block.shape[dim] - width, None, axis...  16.3 us
    scatter-add x1, other arithmetic, deposit(): return dense.at[:, cells].add(values, mode='drop')  14.8 us
    mul x1, other arithmetic, body(): forcing[moment].reshape(tile_rows, columns) * outer  9.62 us
    ppermute x2, starting transfers between devices, swapped(): lax.ppermute(x, axis, [(i, i ^ 1 << apart) for i in range(lax.axis_size(a...  9.26 us
    reshape x2, local copies, waits for them, and re-layouts, ghost_terms(): return target.reshape(fields, layers, central_rows, columns)  8.86 us
  transfers between devices with their start and end apart: 12, of which 3 were waited for; matrix products, arithmetic and copies ran while one was open for 22% of the time, Pallas kernels for 0%

commit v1 on v0

--- a/solution.py
+++ b/solution.py
@@ -2,6 +2,7 @@
 import jax.numpy as jnp
 from jax import lax
 from jax.sharding import PartitionSpec as P
+from jax.lax import all_to_all, axis_size
 
 
 def swapped(x, axis, apart):
@@ -54,7 +55,10 @@
 
 def other_edges(edges):
     across = swapped(edges, "panel", 0)
-    return lax.all_gather(across, "ang", axis=3, tiled=True)
+    return jnp.concatenate(
+        all_to_all(jnp.stack([across for _ in range(axis_size("ang"))], axis=0), "ang", 0, 0),
+        axis=3,
+    )
 
 
 def ghost_terms(scaled_own, row_start, central_rows, ghost_row, ghost_col, ghost_wt):

time: 365 us -> 326 us (0.89)
  blocking collectives: 69.8 us -> 0 us
  starting transfers between devices: 42.5 us -> 55.8 us
  waiting for transfers between devices: 151 us -> 164 us
  local copies, waits for them, and re-layouts: 19.7 us -> 23.5 us
    all_gather x2 -> x0, blocking collectives: 69.8 us -> none  [other_edges(): return lax.all_gather(across, 'ang', axis=3, tiled=True)]
    all_to_all x0 -> x2, starting transfers between devices: none -> 18.7 us  [other_edges(): all_to_all(jnp.stack([across for _ in range(axis_size('ang'))], axis=0),...]
    all_to_all x0 -> x2, waiting for transfers between devices: none -> 11.8 us  [other_edges(): all_to_all(jnp.stack([across for _ in range(axis_size('ang'))], axis=0),...]
    all_to_all x1, starting transfers between devices: 8.52 us -> 4.31 us  [route_obs(): lax.all_to_all(outbox, 'ang', split_axis=1, concat_axis=1, tiled=True)]
  transfers between devices with their start and end apart: 12 -> 14, of which waited for: 3 -> 4; matrix products, arithmetic and copies ran while one was open for 22% -> 26% of each run, Pallas kernels for 0% -> 0%
where the time goes in v1:
time: 326 us; the launch traced here: 325 us
  waiting for transfers between devices  164 us (50%)
  other arithmetic  64.2 us (20%)
  starting transfers between devices  55.8 us (17%)
  local copies, waits for them, and re-layouts  23.5 us (7%)
  between operations  13.8 us (4%)
  matrix products  3.43 us (1%)
    psum x1, waiting for transfers between devices, route_obs(): return lax.psum(dense, 'rad')  151 us
    scatter-add x2, other arithmetic, ghost_terms(): target.at[:, :, flat_index]  31 us
    all_to_all x2, starting transfers between devices, other_edges(): all_to_all(jnp.stack([across for _ in range(axis_size('ang'))], axis=0),...  18.7 us
    ppermute x4, starting transfers between devices, extended(): lax.ppermute(lax.slice_in_dim(block, block.shape[dim] - width, None, axis...  16.5 us
    scatter-add x1, other arithmetic, deposit(): return dense.at[:, cells].add(values, mode='drop')  14.8 us
    all_to_all x2, waiting for transfers between devices, other_edges(): all_to_all(jnp.stack([across for _ in range(axis_size('ang'))], axis=0),...  11.8 us
    mul x1, other arithmetic, body(): forcing[moment].reshape(tile_rows, columns) * outer  9.62 us
    ppermute x2, starting transfers between devices, swapped(): lax.ppermute(x, axis, [(i, i ^ 1 << apart) for i in range(lax.axis_size(a...  9.26 us
  transfers between devices with their start and end apart: 14, of which 4 were waited for; matrix products, arithmetic and copies ran while one was open for 26% of the time, Pallas kernels for 0%

profile of v1, /device:TPU:1, one launch (start us, length us, event | category | flops | bytes accessed | tf_op | source)
XLA Modules:
  0.0 325.1 jit_solution(5549235035172296309)
XLA Ops:
  6.5 1.2 multiply_multiply_fusion.1
  7.8 1.3 collective-permute-start
  9.1 5.5 %collective-permute-start.1 = (f32[7,1,8,1536]{3,0,2,1:T(8,128)S(1)}, f32[7,1,8,1536]{3,0,2,1:T(8,128)S(1)}, u32[]{:S(2)}, u32[]{:S(2)}) collective-permute-start(f32[7,1,8,1536]{3,0,2,1:T(8,128)S(1)} %multiply_multiply_fusion.1), channel_id=1, source_target_pairs={{0,32},{32,64},{64,96},{96,128},{128,160},{160,192},{192,224},{1,3... | collective-permute-start | bytes 1032200 | tf_op jit(solution)/shard_map/ppermute | solution.py:17
  14.6 0.1 copy.94
  14.8 0.1 copy.95
  14.9 4.7 %collective-permute-start.4 = (f32[7,1,2,8]{3,2,0,1:T(2,128)S(1)}, f32[7,1,2,8]{3,2,0,1:T(2,128)S(1)}, u32[]{:S(2)}, u32[]{:S(2)}) collective-permute-start(f32[7,1,2,8]{3,2,0,1:T(2,128)S(1)} %pad_maximum_fusion.18), channel_id=1, source_target_pairs={{0,256},{256,0},{1,257},{257,1},{2,258},{258,2},{3,259},{259,3},{4... | collective-permute-start | bytes 1352 | tf_op jit(solution)/shard_map/ppermute | solution.py:9
  19.6 0.2 fusion.42
  19.8 0.7 add_select_fusion
  20.5 0.7 fusion.37
  21.2 0.6 reduce-window.6
  21.8 0.2 slice_reduce_fusion
  22.0 0.7 convert_bitcast_fusion
  22.7 0.8 fusion.36
  23.5 0.7 broadcast_multiply_fusion
  24.2 0.7 compare_select_fusion.2
  24.9 0.7 stack.9
  25.6 8.5 %all-to-all-start = ((f32[32,7,1,2,8]{4,3,2,1,0:T(2,128)}), f32[32,7,1,2,8]{4,3,2,1,0:T(2,128)S(1)}, u32[]{:S(2)}, u32[]{:S(2)}) async-start(f32[32,7,1,2,8]{4,3,2,1,0:T(2,128)} %stack.9), calls=%async_computation | async-start | bytes 458752 | tf_op jit(solution)/shard_map/all_to_all | solution.py:59
  34.2 1.0 copy.144
  35.1 0.1 copy.103
  35.2 1.3 scatter_fusion
  36.5 0.3 copy.104
  36.8 0.8 reshape.472
  37.5 7.5 %all-to-all-done = f32[32,7,1,2,8]{4,3,2,1,0:T(2,128)S(1)} async-done(((f32[32,7,1,2,8]{4,3,2,1,0:T(2,128)}), f32[32,7,1,2,8]{4,3,2,1,0:T(2,128)S(1)}, u32[]{:S(2)}, u32[]{:S(2)}) %all-to-all-start) | async-done | bytes 14368 | tf_op jit(solution)/shard_map/all_to_all | solution.py:59
  45.0 4.3 %all-to-all-start.1 = ((f32[32,1,192]{2,1,0:T(1,128)}), f32[32,1,192]{2,1,0:T(1,128)S(1)}, u32[]{:S(2)}, u32[]{:S(2)}) async-start(f32[32,1,192]{2,1,0:T(1,128)} %reshape.472), calls=%async_computation.1 | async-start | bytes 65536 | tf_op jit(solution)/shard_map/all_to_all | solution.py:51
  49.4 0.7 copy.133
  50.1 0.4 copy.121
  50.6 15.5 %scatter_custom_fusion = f32[7,12288]{0,1:T(8,128)} fusion(s32[2048]{0:T(1024)S(1)} %bitcast.120, f32[]{:T(128)} %constant.119.clone.1, f32[7,1,2048]{0,2,1:T(8,128)S(1)} %bitcast.96, f32[2048]{0:T(1024)S(1)} %bitcast.110), kind=kCustom, calls=%fused_computation.10 | custom fusion | flops 28672 | bytes 1400836 | tf_op jit(solution)/shard_map/scatter-add | solution.py:75
  66.1 4.4 %copy.99 = f32[7,1,8,1536]{3,0,2,1:T(8,128)S(1)} copy(f32[7,1,8,1536]{0,3,2,1:T(8,128)} %bitcast.94) | data formatting | bytes 688128 | tf_op jit(solution)/shard_map/reshape | solution.py:76
  70.6 0.5 broadcast.330
  71.1 0.7 reduce.14
  71.8 0.1 reshape.473
  72.0 0.1 reshape.442
  72.1 1.4 copy.108
  73.7 0.1 convert_element_type.51
  73.8 14.8 %scatter_custom_fusion.2 = f32[2,12288]{0,1:T(8,128)} fusion(s32[2048]{0:T(1024)S(1)} %bitcast.122, f32[2048,2]{1,0:T(8,128)} %copy.108, f32[]{:T(128)} %constant.119.clone.1), kind=kCustom, calls=%fused_computation.12 | custom fusion | flops 4096 | bytes 98816 | tf_op jit(solution)/shard_map/scatter-add | solution.py:29
  88.7 0.7 pad_maximum_fusion.17
  89.4 2.2 collective-permute-start.2
  91.7 3.6 %collective-permute-start.3 = (f32[7,3,1,1536]{3,0,2,1:T(8,128)S(1)}, f32[7,3,1,1536]{3,0,2,1:T(8,128)S(1)}, u32[]{:S(2)}, u32[]{:S(2)}) collective-permute-start(f32[7,3,1,1536]{3,0,2,1:T(8,128)S(1)} %get-tuple-element.58), channel_id=1, source_target_pairs={{0,1},{1,2},{2,3},{3,4},{4,5},{5,6},{6,7},{7,8},{8,9},{9,10},{10,1... | collective-permute-start | bytes 387080 | tf_op jit(solution)/shard_map/ppermute | solution.py:17
  95.3 151.2 %all-reduce.6.cloned.1.call-done = f32[2,12288]{0,1:T(8,128)} async-done(((f32[2,12288]{0,1:T(8,128)}), f32[2,12288]{0,1:T(8,128)}) %all-reduce.6.cloned.1.call-update) | async-done | bytes 98320 | tf_op jit(solution)/shard_map/psum | solution.py:53
  246.5 9.6 %fusion = (f32[12288]{0:T(1024)S(1)}, f32[12288]{0:T(1024)S(1)}) fusion(f32[2,12288]{0,1:T(8,128)} %all-reduce.6.cloned.1.call-done, f32[]{:T(128)S(6)} %convert_element_type.52), kind=kLoop, calls=%fused_computation.5 | loop fusion | flops 24576 | bytes 196612 | tf_op jit(solution)/shard_map/mul | solution.py:126
  256.2 0.7 copy-done.3
  256.8 1.9 fusion.9
  258.8 0.6 scatter-add.33
  259.4 0.1 multiply_multiply_fusion
  259.5 1.3 collective-permute-start.5
  260.8 4.0 %collective-permute-start.6 = (f32[7,1,8,1536]{3,0,2,1:T(8,128)S(1)}, f32[7,1,8,1536]{3,0,2,1:T(8,128)S(1)}, u32[]{:S(2)}, u32[]{:S(2)}) collective-permute-start(f32[7,1,8,1536]{3,0,2,1:T(8,128)S(1)} %multiply_multiply_fusion), channel_id=1, source_target_pairs={{0,32},{32,64},{64,96},{96,128},{128,160},{160,192},{192,224},{1,3... | collective-permute-start | bytes 1032200 | tf_op jit(solution)/shard_map/ppermute | solution.py:17
  264.9 0.1 copy.110
  265.0 0.1 copy.111
  265.1 4.6 %collective-permute-start.9 = (f32[7,1,2,8]{3,2,0,1:T(2,128)S(1)}, f32[7,1,2,8]{3,2,0,1:T(2,128)S(1)}, u32[]{:S(2)}, u32[]{:S(2)}) collective-permute-start(f32[7,1,2,8]{3,2,0,1:T(2,128)S(1)} %pad_maximum_fusion.19), channel_id=1, source_target_pairs={{0,256},{256,0},{1,257},{257,1},{2,258},{258,2},{3,259},{259,3},{4... | collective-permute-start | bytes 1352 | tf_op jit(solution)/shard_map/ppermute | solution.py:9
  269.8 1.3 collective-permute-done.9
  271.0 0.7 stack.11
  271.8 10.2 %all-to-all-start.2 = ((f32[32,7,1,2,8]{4,3,2,1,0:T(2,128)}), f32[32,7,1,2,8]{4,3,2,1,0:T(2,128)S(1)}, u32[]{:S(2)}, u32[]{:S(2)}) async-start(f32[32,7,1,2,8]{4,3,2,1,0:T(2,128)} %stack.11), calls=%async_computation.2 | async-start | bytes 458752 | tf_op jit(solution)/shard_map/all_to_all | solution.py:59
  282.0 0.8 pad_maximum_fusion.14
  282.7 2.1 collective-permute-start.7
  284.9 3.4 %collective-permute-start.8 = (f32[7,3,1,1536]{3,0,2,1:T(8,128)}, f32[7,3,1,1536]{3,0,2,1:T(8,128)}, u32[]{:S(2)}, u32[]{:S(2)}) collective-permute-start(f32[7,3,1,1536]{3,0,2,1:T(8,128)} %get-tuple-element.56), channel_id=1, source_target_pairs={{0,1},{1,2},{2,3},{3,4},{4,5},{5,6},{6,7},{7,8},{8,9},{9,10},{10,1... | collective-permute-start | bytes 387080 | tf_op jit(solution)/shard_map/ppermute | solution.py:17
  288.3 0.2 fusion.40
  288.5 4.3 %all-to-all-done.2 = f32[32,7,1,2,8]{4,3,2,1,0:T(2,128)S(1)} async-done(((f32[32,7,1,2,8]{4,3,2,1,0:T(2,128)}), f32[32,7,1,2,8]{4,3,2,1,0:T(2,128)S(1)}, u32[]{:S(2)}, u32[]{:S(2)}) %all-to-all-start.2) | async-done | bytes 14368 | tf_op jit(solution)/shard_map/all_to_all | solution.py:59
  292.8 1.1 copy.125
  294.0 1.0 mul.234
  295.0 15.5 %scatter_custom_fusion.3 = f32[7,12288]{0,1:T(8,128)} fusion(s32[2048]{0:T(1024)S(1)} %bitcast.121, f32[]{:T(128)} %constant.119.clone.1, f32[7,1,2048]{0,2,1:T(8,128)S(1)} %bitcast.95, f32[2048]{0:T(1024)S(1)} %bitcast.111), kind=kCustom, calls=%fused_computation.8 | custom fusion | flops 28672 | bytes 1400836 | tf_op jit(solution)/shard_map/scatter-add | solution.py:75
  310.5 4.4 %copy.115 = f32[7,1,8,1536]{3,0,2,1:T(8,128)S(1)} copy(f32[7,1,8,1536]{0,3,2,1:T(8,128)} %bitcast.93) | data formatting | bytes 688128 | tf_op jit(solution)/shard_map/reshape | solution.py:76
  314.9 1.6 fusion.8
  316.6 0.6 scatter-add.35
  317.3 0.9 copy.118
  (43 shorter events, 0.9 us)
Async XLA Ops:
  6.5 250.3 %copy-start = (f32[7,7]{1,0:T(8,128)S(1)}, f32[7,7]{1,0:T(8,128)}, u32[]{:S(2)}) copy-start(f32[7,7]{1,0:T(8,128)} %param.22) | copy-start | bytes 592
  7.8 80.9 %collective-permute-start = (f32[7,1,8,1536]{3,0,2,1:T(8,128)S(1)}, f32[7,1,8,1536]{3,0,2,1:T(8,128)S(1)}, u32[]{:S(2)}, u32[]{:S(2)}) collective-permute-start(f32[7,1,8,1536]{3,0,2,1:T(8,128)S(1)} %multiply_multiply_fusion.1), channel_id=1, source_target_pairs={{32,0},{64,32},{96,64},{128,96},{160,128},{192,160},{224,192},{33,... | collective-permute-start | bytes 1032200 | tf_op jit(solution)/shard_map/ppermute | solution.py:20
  9.1 79.6 %collective-permute-start.1 = (f32[7,1,8,1536]{3,0,2,1:T(8,128)S(1)}, f32[7,1,8,1536]{3,0,2,1:T(8,128)S(1)}, u32[]{:S(2)}, u32[]{:S(2)}) collective-permute-start(f32[7,1,8,1536]{3,0,2,1:T(8,128)S(1)} %multiply_multiply_fusion.1), channel_id=1, source_target_pairs={{0,32},{32,64},{64,96},{96,128},{128,160},{160,192},{192,224},{1,3... | collective-permute-start | bytes 1032200 | tf_op jit(solution)/shard_map/ppermute | solution.py:17
  14.9 10.0 %collective-permute-start.4 = (f32[7,1,2,8]{3,2,0,1:T(2,128)S(1)}, f32[7,1,2,8]{3,2,0,1:T(2,128)S(1)}, u32[]{:S(2)}, u32[]{:S(2)}) collective-permute-start(f32[7,1,2,8]{3,2,0,1:T(2,128)S(1)} %pad_maximum_fusion.18), channel_id=1, source_target_pairs={{0,256},{256,0},{1,257},{257,1},{2,258},{258,2},{3,259},{259,3},{4... | collective-permute-start | bytes 1352 | tf_op jit(solution)/shard_map/ppermute | solution.py:9
  25.6 19.4 %all-to-all-start = ((f32[32,7,1,2,8]{4,3,2,1,0:T(2,128)}), f32[32,7,1,2,8]{4,3,2,1,0:T(2,128)S(1)}, u32[]{:S(2)}, u32[]{:S(2)}) async-start(f32[32,7,1,2,8]{4,3,2,1,0:T(2,128)} %stack.9), calls=%async_computation | async-start | bytes 458752 | tf_op jit(solution)/shard_map/all_to_all | solution.py:59
  45.0 25.5 %all-to-all-start.1 = ((f32[32,1,192]{2,1,0:T(1,128)}), f32[32,1,192]{2,1,0:T(1,128)S(1)}, u32[]{:S(2)}, u32[]{:S(2)}) async-start(f32[32,1,192]{2,1,0:T(1,128)} %reshape.472), calls=%async_computation.1 | async-start | bytes 65536 | tf_op jit(solution)/shard_map/all_to_all | solution.py:51
  49.3 197.2 %all-reduce.6.cloned.1.call-start = ((), (), s32[]{:S(2)}) async-start(), calls=%async_computation.3 | async-start | bytes 12582912 | tf_op jit(solution)/shard_map/psum | solution.py:53
  89.4 166.7 %collective-permute-start.2 = (f32[7,3,1,1536]{3,0,2,1:T(8,128)}, f32[7,3,1,1536]{3,0,2,1:T(8,128)S(1)}, u32[]{:S(2)}, u32[]{:S(2)}) collective-permute-start(f32[7,3,1,1536]{3,0,2,1:T(8,128)} %get-tuple-element.57), channel_id=1, source_target_pairs={{1,0},{2,1},{3,2},{4,3},{5,4},{6,5},{7,6},{8,7},{9,8},{10,9},{11,1... | collective-permute-start | bytes 387080 | tf_op jit(solution)/shard_map/ppermute | solution.py:20
  91.6 165.2 %copy-start.1 = (f32[1,7,1,8,1536]{4,3,2,1,0:T(8,128)S(1)}, f32[1,7,1,8,1536]{4,3,2,1,0:T(8,128)}, u32[]{:S(2)}) copy-start(f32[1,7,1,8,1536]{4,3,2,1,0:T(8,128)} %param.19) | copy-start | bytes 1032196
  91.7 167.7 %copy-start.2 = (f32[1,1,8,1536]{3,2,1,0:T(8,128)S(1)}, f32[1,1,8,1536]{3,2,1,0:T(8,128)}, u32[]{:S(2)}) copy-start(f32[1,1,8,1536]{3,2,1,0:T(8,128)} %param.20) | copy-start | bytes 147460
  91.7 167.7 %copy-start.4 = (f32[7]{0:T(128)S(1)}, f32[7]{0:T(128)}, u32[]{:S(2)}) copy-start(f32[7]{0:T(128)} %param.21) | copy-start | bytes 88
  91.7 164.5 %collective-permute-start.3 = (f32[7,3,1,1536]{3,0,2,1:T(8,128)S(1)}, f32[7,3,1,1536]{3,0,2,1:T(8,128)S(1)}, u32[]{:S(2)}, u32[]{:S(2)}) collective-permute-start(f32[7,3,1,1536]{3,0,2,1:T(8,128)S(1)} %get-tuple-element.58), channel_id=1, source_target_pairs={{0,1},{1,2},{2,3},{3,4},{4,5},{5,6},{6,7},{7,8},{8,9},{9,10},{10,1... | collective-permute-start | bytes 387080 | tf_op jit(solution)/shard_map/ppermute | solution.py:17
  256.1 0.7 copy-start.3
  259.5 22.5 %collective-permute-start.5 = (f32[7,1,8,1536]{3,0,2,1:T(8,128)S(1)}, f32[7,1,8,1536]{3,0,2,1:T(8,128)S(1)}, u32[]{:S(2)}, u32[]{:S(2)}) collective-permute-start(f32[7,1,8,1536]{3,0,2,1:T(8,128)S(1)} %multiply_multiply_fusion), channel_id=1, source_target_pairs={{32,0},{64,32},{96,64},{128,96},{160,128},{192,160},{224,192},{33,... | collective-permute-start | bytes 1032200 | tf_op jit(solution)/shard_map/ppermute | solution.py:20
  260.8 21.2 %collective-permute-start.6 = (f32[7,1,8,1536]{3,0,2,1:T(8,128)S(1)}, f32[7,1,8,1536]{3,0,2,1:T(8,128)S(1)}, u32[]{:S(2)}, u32[]{:S(2)}) collective-permute-start(f32[7,1,8,1536]{3,0,2,1:T(8,128)S(1)} %multiply_multiply_fusion), channel_id=1, source_target_pairs={{0,32},{32,64},{64,96},{96,128},{128,160},{160,192},{192,224},{1,3... | collective-permute-start | bytes 1032200 | tf_op jit(solution)/shard_map/ppermute | solution.py:17
  265.1 5.9 %collective-permute-start.9 = (f32[7,1,2,8]{3,2,0,1:T(2,128)S(1)}, f32[7,1,2,8]{3,2,0,1:T(2,128)S(1)}, u32[]{:S(2)}, u32[]{:S(2)}) collective-permute-start(f32[7,1,2,8]{3,2,0,1:T(2,128)S(1)} %pad_maximum_fusion.19), channel_id=1, source_target_pairs={{0,256},{256,0},{1,257},{257,1},{2,258},{258,2},{3,259},{259,3},{4... | collective-permute-start | bytes 1352 | tf_op jit(solution)/shard_map/ppermute | solution.py:9
  271.8 21.0 %all-to-all-start.2 = ((f32[32,7,1,2,8]{4,3,2,1,0:T(2,128)}), f32[32,7,1,2,8]{4,3,2,1,0:T(2,128)S(1)}, u32[]{:S(2)}, u32[]{:S(2)}) async-start(f32[32,7,1,2,8]{4,3,2,1,0:T(2,128)} %stack.11), calls=%async_computation.2 | async-start | bytes 458752 | tf_op jit(solution)/shard_map/all_to_all | solution.py:59
  282.7 32.2 %collective-permute-start.7 = (f32[7,3,1,1536]{3,0,2,1:T(8,128)}, f32[7,3,1,1536]{3,0,2,1:T(8,128)}, u32[]{:S(2)}, u32[]{:S(2)}) collective-permute-start(f32[7,3,1,1536]{3,0,2,1:T(8,128)} %get-tuple-element.55), channel_id=1, source_target_pairs={{1,0},{2,1},{3,2},{4,3},{5,4},{6,5},{7,6},{8,7},{9,8},{10,9},{11,1... | collective-permute-start | bytes 387080 | tf_op jit(solution)/shard_map/ppermute | solution.py:20
  284.9 30.0 %collective-permute-start.8 = (f32[7,3,1,1536]{3,0,2,1:T(8,128)}, f32[7,3,1,1536]{3,0,2,1:T(8,128)}, u32[]{:S(2)}, u32[]{:S(2)}) collective-permute-start(f32[7,3,1,1536]{3,0,2,1:T(8,128)} %get-tuple-element.56), channel_id=1, source_target_pairs={{0,1},{1,2},{2,3},{3,4},{4,5},{5,6},{6,7},{7,8},{8,9},{9,10},{10,1... | collective-permute-start | bytes 387080 | tf_op jit(solution)/shard_map/ppermute | solution.py:17
Sparse Core Ops, SparseCore 0:
  88.8 157.6 all-reduce.5
